TPU v7x, 256 devices: a whole 4x4x8 slice. The times are simulated.
256 devices in a mesh: section: 8 (over z_lo, core), dp: 32 (over y, x, z_hi).
Axes of the slice: x: 4, y: 4, z: 8 (z_hi: 2, z_lo: 4; z = z_hi * 4 + z_lo), core: 2. Of those that a mesh axis runs over, the one named last changes fastest.
Arguments:
- clips: bfloat16 [8, 32, 4, 8, 8, 128], P(None, 'dp'), may hold values from -6 to 6
- cotangent: bfloat16 [8, 32, 4, 8, 8, 128], P(None, 'dp'), may hold values from -6 to 6
- weights: bfloat16 [8, 3456, 128], P('section', 'dp'), may hold values from -0.078125 to 0.078125
Outputs:
- section_outs: bfloat16 [8, 8, 32, 4, 8, 8, 128], P('section', None, 'dp')
- weight_grads: float32 [8, 3456, 128], P('section', 'dp')
All inputs are finite; a program needn't handle non-finite values.
Results may differ from a plain program's by a relative error of at most 0.027.
Values may be sent and summed in bfloat16 or wider, within the bound.
A program may use at most 64 MiB of HBM per device.

v0:
```python
import jax
import jax.numpy as jnp
from jax import lax
from jax.sharding import PartitionSpec as P


def passed_along(block, axis, distance):
    devices = range(lax.axis_size(axis))
    route = [(i - distance, i) for i in devices if i - distance in devices]
    return lax.ppermute(block, axis, route)


def gather_patches(field):
    frames, height, width, channels = field.shape
    first_frame = field[:1]
    padded = jnp.concatenate([first_frame, first_frame, field], axis=0)
    padded = jnp.pad(padded, ((0, 0), (1, 1), (1, 1), (0, 0)))
    pieces = [
        padded[
            offset_time : offset_time + frames,
            offset_row : offset_row + height,
            offset_col : offset_col + width,
        ]
        for offset_time in range(3)
        for offset_row in range(3)
        for offset_col in range(3)
    ]
    return jnp.stack(pieces, axis=3).reshape(frames * height * width, 27 * channels)


def squash_field(activation):
    return jax.nn.silu(activation.astype(jnp.float32)).astype(jnp.bfloat16)


def squash_columns(activation):
    return gather_patches(squash_field(activation))


def layer_forward(activation, weight):
    branch = jnp.dot(squash_columns(activation), weight, preferred_element_type=jnp.float32)
    return (activation.astype(jnp.float32) + branch.reshape(activation.shape)).astype(jnp.bfloat16)


def input_gradient(activation, upstream, weight):
    flat_grad = upstream.reshape(-1, weight.shape[1])
    column_grad = lax.dot_general(
        flat_grad, weight, (((1,), (1,)), ((), ())), preferred_element_type=jnp.float32
    )
    base = activation.astype(jnp.float32)
    _, unfold = jax.vjp(gather_patches, base)
    field_grad = unfold(column_grad)[0]
    sigmoid_value = jax.nn.sigmoid(base)
    slope = sigmoid_value * (1.0 + base * (1.0 - sigmoid_value))
    return (upstream.astype(jnp.float32) + field_grad * slope).astype(jnp.bfloat16)


def weight_term(activation, upstream):
    flat_grad = upstream.reshape(-1, upstream.shape[-1])
    return lax.dot_general(
        squash_columns(activation),
        flat_grad,
        (((0,), (0,)), ((), ())),
        preferred_element_type=jnp.float32,
    )


def per_device(clips, cotangent, weights):
    section_total = lax.axis_size("section")
    section_index = lax.axis_index("section")
    weight = lax.all_gather(weights, "dp", axis=1, tiled=True)[0]
    local_clips = clips[:, 0]
    local_grads = cotangent[:, 0]
    micro_count = local_clips.shape[0]
    step_count = micro_count + section_total - 1
    empty_field = jnp.zeros(local_clips.shape[1:], jnp.bfloat16)

    def forward_step(step_index, carry):
        received, saved_inputs, produced = carry
        micro_index = step_index - section_index
        active = (micro_index >= 0) & (micro_index < micro_count)
        slot_index = jnp.clip(micro_index, 0, micro_count - 1)
        fresh = lax.dynamic_index_in_dim(local_clips, slot_index, 0, keepdims=False)
        layer_input = jnp.where(section_index == 0, fresh, received)
        layer_output = layer_forward(layer_input, weight)
        kept_input = jnp.where(
            active,
            layer_input,
            lax.dynamic_index_in_dim(saved_inputs, slot_index, 0, keepdims=False),
        )
        kept_output = jnp.where(
            active, layer_output, lax.dynamic_index_in_dim(produced, slot_index, 0, keepdims=False)
        )
        saved_inputs = lax.dynamic_update_index_in_dim(saved_inputs, kept_input, slot_index, 0)
        produced = lax.dynamic_update_index_in_dim(produced, kept_output, slot_index, 0)
        received = passed_along(layer_output, "section", 1)
        return (received, saved_inputs, produced)

    start_forward = (empty_field, jnp.zeros_like(local_clips), jnp.zeros_like(local_clips))
    _, saved_inputs, produced = lax.fori_loop(0, step_count, forward_step, start_forward)

    def backward_step(step_index, carry):
        received, grad_total, kept_grads = carry
        micro_index = step_index - (section_total - 1 - section_index)
        active = (micro_index >= 0) & (micro_index < micro_count)
        slot_index = jnp.clip(micro_index, 0, micro_count - 1)
        fresh = lax.dynamic_index_in_dim(local_grads, slot_index, 0, keepdims=False)
        upstream = jnp.where(section_index == section_total - 1, fresh, received)
        activation = lax.dynamic_index_in_dim(saved_inputs, slot_index, 0, keepdims=False)
        grad_total = grad_total + jnp.where(active, weight_term(activation, upstream), 0.0)
        layer_grad = input_gradient(activation, upstream, weight)
        received = passed_along(layer_grad, "section", -1)
        return (received, grad_total, kept_grads)

    start_backward = (
        empty_field,
        jnp.zeros(weight.shape, jnp.float32),
        jnp.zeros_like(local_grads),
    )
    _, grad_total, kept_grads = lax.fori_loop(0, step_count, backward_step, start_backward)
    grad_share = lax.psum_scatter(
        grad_total.astype(jnp.bfloat16), "dp", scatter_dimension=0, tiled=True
    ).astype(jnp.float32)
    return (produced[None, :, None], grad_share[None])


def solution(mesh):
    placed = (
        P(None, "dp", None, None, None, None),
        P(None, "dp", None, None, None, None),
        P("section", "dp", None),
    )
    return jax.shard_map(
        per_device,
        mesh=mesh,
        in_specs=placed,
        out_specs=(P("section", None, "dp", None, None, None, None), P("section", "dp", None)),
        check_vma=False,
    )
```

profile of v0, /device:TPU:98, one launch (start us, length us, event | category | flops | bytes accessed | tf_op | source)
XLA Modules:
  0.0 626.4 jit_solution(11397557660246506297)
XLA Ops:
  1.4 153.5 %all_gather.3 = bf16[1,3456,128]{2,0,1:T(2,128)(2,1)S(1)} all-gather(bf16[1,108,128]{2,0,1:T(2,128)(2,1)S(1)} %copy.118), channel_id=1, replica_groups=mesh['section'=8,'dp'=32] {'dp'}, dimensions={1}, use_global_device_ids=true | all-gather | bytes 912384 | tf_op jit(solution)/shard_map/all_gather | solution.py:70
  157.0 159.6 %while.37 = (s32[]{:T(128)}, bf16[4,8,8,128]{3,2,1,0:T(8,128)(2,1)S(1)}, bf16[8,4,8,8,128]{4,3,2,1,0:T(8,128)(2,1)}, bf16[8,4,8,8,128]{4,3,2,1,0:T(8,128)(2,1)S(...) while((s32[]{:T(128)}, ...), condition=%wide.region_1.2_spmd, body=%wide.region_0.1_spmd.sunk | while | flops 227311616 | bytes 8454884 | solution.py:99
  164.0 3.7 collective-permute-done
  174.7 3.7 collective-permute-done
  185.3 3.7 collective-permute-done
  196.0 3.7 collective-permute-done
  206.6 3.7 collective-permute-done
  217.3 3.7 collective-permute-done
  227.9 3.7 collective-permute-done
  238.5 3.7 collective-permute-done
  249.2 3.7 collective-permute-done
  259.8 3.7 collective-permute-done
  270.4 3.7 collective-permute-done
  281.1 3.7 collective-permute-done
  291.7 3.7 collective-permute-done
  302.3 3.7 collective-permute-done
  313.0 3.7 collective-permute-done
  317.4 174.1 %while.38 = (s32[]{:T(128)}, bf16[4,8,8,128]{3,2,1,0:T(8,128)(2,1)}, f32[3456,128]{1,0:T(8,128)S(1)}, pred[]{:T(512)}, s32[]{:T(128)}, /*index=5*/bf16[8,4,8,8,1...) while((s32[]{:T(128)}, ...), condition=%wide.region_3.4_spmd.clone, body=%wide.region_2.3_spmd.clone.sunk | while | flops 457267200 | bytes 30126344 | solution.py:119
  322.7 3.1 collective-permute-start.1
  327.8 2.0 fusion.264
  335.2 4.8 collective-permute-start.1
  342.0 2.0 fusion.264
  353.3 2.0 fusion.264
  360.7 2.6 collective-permute-start.1
  365.3 2.0 fusion.264
  387.9 2.0 fusion.264
  410.5 2.0 fusion.264
  444.4 2.0 fusion.264
  466.9 2.0 fusion.264
  489.5 2.0 fusion.264
  491.7 123.0 %fusion = bf16[112,128]{1,0:T(8,128)(2,1)S(1)} fusion(bf16[3456,128]{1,0:T(8,128)(2,1)S(1)} %convert_element_type.115), kind=kCustom, calls=%all-reduce-scatter | all-reduce-scatter fusion | flops 458753 | bytes 914432
  619.8 4.5 collective-permute-done.3
  (1148 shorter events, 255.8 us)
Async XLA Ops:
  162.1 5.6 collective-permute-start
  172.8 5.6 collective-permute-start
  183.4 5.6 collective-permute-start
  194.0 5.6 collective-permute-start
  204.7 5.6 collective-permute-start
  215.3 5.6 collective-permute-start
  226.0 5.6 collective-permute-start
  236.6 5.6 collective-permute-start
  247.2 5.6 collective-permute-start
  257.9 5.6 collective-permute-start
  268.5 5.6 collective-permute-start
  279.1 5.6 collective-permute-start
  289.8 5.6 collective-permute-start
  300.4 5.6 collective-permute-start
  311.0 5.6 collective-permute-start
  322.7 7.1 %collective-permute-start.1 = (bf16[4,8,8,128]{3,2,1,0:T(8,128)(2,1)}, bf16[4,8,8,128]{3,2,1,0:T(8,128)(2,1)}, u32[]{:S(2)}, u32[]{:S(2)}) collective-permute-start(bf16[4,8,8,128]{3,2,1,0:T(8,128)(2,1)} %get-tuple-element.632), channel_id=1, source_target_pairs={{32,0},{64,32},{96,64},{128,96},{160,128},{192,160},{224,192},{33,... | collective-permute-start | bytes 196616 | tf_op jit(solution)/shard_map/while/body/eval_jaxpr/ppermute | solution.py:10
  335.2 8.9 %collective-permute-start.1 = (bf16[4,8,8,128]{3,2,1,0:T(8,128)(2,1)}, bf16[4,8,8,128]{3,2,1,0:T(8,128)(2,1)}, u32[]{:S(2)}, u32[]{:S(2)}) collective-permute-start(bf16[4,8,8,128]{3,2,1,0:T(8,128)(2,1)} %get-tuple-element.632), channel_id=1, source_target_pairs={{32,0},{64,32},{96,64},{128,96},{160,128},{192,160},{224,192},{33,... | collective-permute-start | bytes 196616 | tf_op jit(solution)/shard_map/while/body/eval_jaxpr/ppermute | solution.py:10
  349.4 6.0 collective-permute-start.1
  360.7 6.7 %collective-permute-start.1 = (bf16[4,8,8,128]{3,2,1,0:T(8,128)(2,1)}, bf16[4,8,8,128]{3,2,1,0:T(8,128)(2,1)}, u32[]{:S(2)}, u32[]{:S(2)}) collective-permute-start(bf16[4,8,8,128]{3,2,1,0:T(8,128)(2,1)} %get-tuple-element.632), channel_id=1, source_target_pairs={{32,0},{64,32},{96,64},{128,96},{160,128},{192,160},{224,192},{33,... | collective-permute-start | bytes 196616 | tf_op jit(solution)/shard_map/while/body/eval_jaxpr/ppermute | solution.py:10
  372.7 6.0 collective-permute-start.1
  384.0 6.0 collective-permute-start.1
  395.3 6.0 collective-permute-start.1
  406.6 6.0 collective-permute-start.1
  417.8 6.0 collective-permute-start.1
  429.1 6.0 collective-permute-start.1
  440.4 6.0 collective-permute-start.1
  451.7 6.0 collective-permute-start.1
  463.0 6.0 collective-permute-start.1
  474.3 6.0 collective-permute-start.1
  485.6 6.0 collective-permute-start.1
  614.7 10.6 %collective-permute-start.2 = (bf16[112,128]{1,0:T(8,128)(2,1)S(1)}, bf16[112,128]{1,0:T(8,128)(2,1)S(1)}, u32[]{:S(2)}, u32[]{:S(2)}) collective-permute-start(bf16[112,128]{1,0:T(8,128)(2,1)S(1)} %fusion), channel_id=1, source_target_pairs={{0,1},{1,2},{2,3},{3,4},{4,5},{5,6},{6,7},{7,8},{8,9},{9,10},{10,1... | collective-permute-start | bytes 86024
  616.6 7.7 %collective-permute-start.3 = (bf16[12,128]{1,0:T(8,128)(2,1)S(1)}, bf16[12,128]{1,0:T(8,128)(2,1)S(1)}, u32[]{:S(2)}, u32[]{:S(2)}) collective-permute-start(bf16[12,128]{1,0:T(8,128)(2,1)S(1)} %slice.589), channel_id=1, source_target_pairs={{0,2},{1,3},{2,4},{3,5},{4,6},{5,7},{6,8},{7,9},{8,10},{9,11},{10,... | collective-permute-start | bytes 9224
  (17 other events, 170.4 us)
where the time goes:
time: 633 us; the launch traced here: 626 us
  blocking collectives  276 us (44%)
  matrix products  85.5 us (14%)
  other arithmetic  82.8 us (13%)
  starting transfers between devices  66.2 us (10%)
  waiting for transfers between devices  60.3 us (10%)
  local copies, waits for them, and re-layouts  49.3 us (8%)
    all_gather x1, blocking collectives, per_device(): weight = lax.all_gather(weights, 'dp', axis=1, tiled=True)[0]  153 us
    unnamed x1, blocking collectives  123 us
    ppermute x30, starting transfers between devices, passed_along(): return lax.ppermute(block, axis, route)  62.3 us
    ppermute x30, waiting for transfers between devices, passed_along(): return lax.ppermute(block, axis, route)  54.8 us
    dot_general x15, matrix products, weight_term(): lax.dot_general(squash_columns(activation), flat_grad, (((0,), (0,)), (()...  30.6 us
    dot_general x15, matrix products, layer_forward(): jnp.dot(squash_columns(activation), weight, preferred_element_type=jnp.fl...  27.5 us
    dot_general x15, matrix products, input_gradient(): lax.dot_general(flat_grad, weight, (((1,), (1,)), ((), ())), preferred_el...  27.4 us
    convert_element_type x30, other arithmetic, squash_field(): return jax.nn.silu(activation.astype(jnp.float32)).astype(jnp.bfloat16)  23.9 us
  transfers between devices with their start and end apart: 32, of which 17 were waited for; matrix products, arithmetic and copies ran while one was open for 10% of the time, Pallas kernels for 0%

commit v1 on v0

--- a/solution.py
+++ b/solution.py
@@ -2,6 +2,11 @@
 import jax.numpy as jnp
 from jax import lax
 from jax.sharding import PartitionSpec as P
+
+
+def swapped_in(block, mesh_axis, dim):
+    stack = jnp.stack([block] * lax.axis_size(mesh_axis))
+    return jnp.concatenate(lax.all_to_all(stack, mesh_axis, 0, 0), axis=dim)
 
 
 def passed_along(block, axis, distance):
@@ -67,7 +72,7 @@
 def per_device(clips, cotangent, weights):
     section_total = lax.axis_size("section")
     section_index = lax.axis_index("section")
-    weight = lax.all_gather(weights, "dp", axis=1, tiled=True)[0]
+    weight = swapped_in(weights, "dp", 1)[0]
     local_clips = clips[:, 0]
     local_grads = cotangent[:, 0]
     micro_count = local_clips.shape[0]

time: 633 us -> 517 us (0.82)
  blocking collectives: 276 us -> 121 us
  waiting for transfers between devices: 60.3 us -> 87.3 us
  starting transfers between devices: 66.2 us -> 77.1 us
    all_gather x1 -> x0, blocking collectives: 153 us -> none  [per_device(): weight = lax.all_gather(weights, 'dp', axis=1, tiled=True)[0]]
    all_to_all x0 -> x1, waiting for transfers between devices: none -> 21.6 us  [swapped_in(): return jnp.concatenate(lax.all_to_all(stack, mesh_axis, 0, 0), axis=dim)]
    all_to_all x0 -> x1, starting transfers between devices: none -> 11.5 us  [swapped_in(): return jnp.concatenate(lax.all_to_all(stack, mesh_axis, 0, 0), axis=dim)]
  transfers between devices with their start and end apart: 32 -> 33, of which waited for: 17 -> 18; matrix products, arithmetic and copies ran while one was open for 10% -> 12% of each run, Pallas kernels for 0% -> 0%
where the time goes in v1:
time: 517 us; the launch traced here: 510 us
  blocking collectives  121 us (23%)
  waiting for transfers between devices  87.3 us (17%)
  matrix products  85.5 us (17%)
  other arithmetic  82.7 us (16%)
  starting transfers between devices  77.1 us (15%)
  local copies, waits for them, and re-layouts  50.3 us (10%)
    unnamed x1, blocking collectives  121 us
    ppermute x30, starting transfers between devices, passed_along(): return lax.ppermute(block, axis, route)  61.7 us
    ppermute x30, waiting for transfers between devices, passed_along(): return lax.ppermute(block, axis, route)  60.1 us
    dot_general x15, matrix products, weight_term(): lax.dot_general(squash_columns(activation), flat_grad, (((0,), (0,)), (()...  30.6 us
    dot_general x15, matrix products, layer_forward(): jnp.dot(squash_columns(activation), weight, preferred_element_type=jnp.fl...  27.5 us
    dot_general x15, matrix products, input_gradient(): lax.dot_general(flat_grad, weight, (((1,), (1,)), ((), ())), preferred_el...  27.4 us
    convert_element_type x30, other arithmetic, squash_field(): return jax.nn.silu(activation.astype(jnp.float32)).astype(jnp.bfloat16)  24 us
    dynamic_update_slice x15, other arithmetic, forward_step(): lax.dynamic_update_index_in_dim(saved_inputs, kept_input, slot_index, 0)  22.4 us
  transfers between devices with their start and end apart: 33, of which 18 were waited for; matrix products, arithmetic and copies ran while one was open for 12% of the time, Pallas kernels for 0%

profile of v1, /device:TPU:98, one launch (start us, length us, event | category | flops | bytes accessed | tf_op | source)
XLA Modules:
  0.0 510.2 jit_solution(8583848477120478737)
XLA Ops:
  2.4 11.5 %all-to-all-start = ((bf16[32,1,108,128]{3,2,1,0:T(8,128)(2,1)}), bf16[32,1,108,128]{3,2,1,0:T(8,128)(2,1)S(1)}, u32[]{:S(2)}, u32[]{:S(2)}) async-start(bf16[32,1,108,128]{3,2,1,0:T(8,128)(2,1)} %stack.591), calls=%async_computation | async-start | bytes 1835008 | tf_op jit(solution)/shard_map/all_to_all | solution.py:9
  14.0 21.6 %all-to-all-done = bf16[32,1,108,128]{3,2,1,0:T(8,128)(2,1)S(1)} async-done(((bf16[32,1,108,128]{3,2,1,0:T(8,128)(2,1)}), bf16[32,1,108,128]{3,2,1,0:T(8,128)(2,1)S(1)}, u32[]{:S(2)}, u32[]{:S(2)}) %all-to-all-start) | async-done | bytes 884768 | tf_op jit(solution)/shard_map/all_to_all | solution.py:9
  37.7 164.7 %while.37 = (s32[]{:T(128)}, bf16[4,8,8,128]{3,2,1,0:T(8,128)(2,1)S(1)}, bf16[8,4,8,8,128]{4,3,2,1,0:T(8,128)(2,1)}, bf16[8,4,8,8,128]{4,3,2,1,0:T(8,128)(2,1)S(...) while((s32[]{:T(128)}, ...), condition=%wide.region_1.2_spmd, body=%wide.region_0.1_spmd.sunk | while | flops 227311616 | bytes 8454884 | solution.py:104
  44.7 8.9 %collective-permute-done = bf16[4,8,8,128]{3,2,1,0:T(8,128)(2,1)S(1)} collective-permute-done((bf16[4,8,8,128]{3,2,1,0:T(8,128)(2,1)S(1)}, bf16[4,8,8,128]{3,2,1,0:T(8,128)(2,1)S(1)}, u32[]{:S(2)}, u32[]{:S(2)}) %collective-permute-start) | collective-permute-done | bytes 65568 | tf_op jit(solution)/shard_map/while/body/eval_jaxpr/ppermute | solution.py:15
  60.6 3.7 collective-permute-done
  71.3 3.7 collective-permute-done
  81.9 3.7 collective-permute-done
  92.5 3.7 collective-permute-done
  103.1 3.7 collective-permute-done
  113.8 3.7 collective-permute-done
  124.4 3.7 collective-permute-done
  135.0 3.7 collective-permute-done
  145.7 3.7 collective-permute-done
  156.3 3.7 collective-permute-done
  166.9 3.7 collective-permute-done
  177.6 3.7 collective-permute-done
  188.2 3.7 collective-permute-done
  198.8 3.7 collective-permute-done
  203.3 173.7 %while.38 = (s32[]{:T(128)}, bf16[4,8,8,128]{3,2,1,0:T(8,128)(2,1)}, f32[3456,128]{1,0:T(8,128)S(1)}, pred[]{:T(512)}, s32[]{:T(128)}, /*index=5*/bf16[8,4,8,8,1...) while((s32[]{:T(128)}, ...), condition=%wide.region_3.4_spmd.clone, body=%wide.region_2.3_spmd.clone.sunk | while | flops 457267200 | bytes 30126344 | solution.py:124
  208.6 2.1 collective-permute-start.1
  212.7 2.0 fusion.264
  220.1 4.8 collective-permute-start.1
  226.9 2.0 fusion.264
  238.2 2.0 fusion.264
  245.6 3.0 collective-permute-start.1
  250.6 2.0 fusion.264
  261.9 2.0 fusion.264
  284.5 2.0 fusion.264
  352.3 2.0 fusion.264
  363.6 2.0 fusion.264
  377.1 121.3 %fusion = bf16[112,128]{1,0:T(8,128)(2,1)S(1)} fusion(bf16[3456,128]{1,0:T(8,128)(2,1)S(1)} %convert_element_type.115), kind=kCustom, calls=%all-reduce-scatter | all-reduce-scatter fusion | flops 458753 | bytes 914432
  503.5 4.4 collective-permute-done.3
  (1149 shorter events, 259.0 us)
Async XLA Ops:
  2.4 33.2 %all-to-all-start = ((bf16[32,1,108,128]{3,2,1,0:T(8,128)(2,1)}), bf16[32,1,108,128]{3,2,1,0:T(8,128)(2,1)S(1)}, u32[]{:S(2)}, u32[]{:S(2)}) async-start(bf16[32,1,108,128]{3,2,1,0:T(8,128)(2,1)} %stack.591), calls=%async_computation | async-start | bytes 1835008 | tf_op jit(solution)/shard_map/all_to_all | solution.py:9
  42.8 10.9 %collective-permute-start = (bf16[4,8,8,128]{3,2,1,0:T(8,128)(2,1)S(1)}, bf16[4,8,8,128]{3,2,1,0:T(8,128)(2,1)S(1)}, u32[]{:S(2)}, u32[]{:S(2)}) collective-permute-start(bf16[4,8,8,128]{3,2,1,0:T(8,128)(2,1)S(1)} %get-tuple-element.592), channel_id=1, source_target_pairs={{0,32},{32,64},{64,96},{96,128},{128,160},{160,192},{192,224},{1,3... | collective-permute-start | bytes 196616 | tf_op jit(solution)/shard_map/while/body/eval_jaxpr/ppermute | solution.py:15
  58.7 5.6 %collective-permute-start = (bf16[4,8,8,128]{3,2,1,0:T(8,128)(2,1)S(1)}, bf16[4,8,8,128]{3,2,1,0:T(8,128)(2,1)S(1)}, u32[]{:S(2)}, u32[]{:S(2)}) collective-permute-start(bf16[4,8,8,128]{3,2,1,0:T(8,128)(2,1)S(1)} %get-tuple-element.592), channel_id=1, source_target_pairs={{0,32},{32,64},{64,96},{96,128},{128,160},{160,192},{192,224},{1,3... | collective-permute-start | bytes 196616 | tf_op jit(solution)/shard_map/while/body/eval_jaxpr/ppermute | solution.py:15
  69.3 5.6 %collective-permute-start = (bf16[4,8,8,128]{3,2,1,0:T(8,128)(2,1)S(1)}, bf16[4,8,8,128]{3,2,1,0:T(8,128)(2,1)S(1)}, u32[]{:S(2)}, u32[]{:S(2)}) collective-permute-start(bf16[4,8,8,128]{3,2,1,0:T(8,128)(2,1)S(1)} %get-tuple-element.592), channel_id=1, source_target_pairs={{0,32},{32,64},{64,96},{96,128},{128,160},{160,192},{192,224},{1,3... | collective-permute-start | bytes 196616 | tf_op jit(solution)/shard_map/while/body/eval_jaxpr/ppermute | solution.py:15
  80.0 5.6 %collective-permute-start = (bf16[4,8,8,128]{3,2,1,0:T(8,128)(2,1)S(1)}, bf16[4,8,8,128]{3,2,1,0:T(8,128)(2,1)S(1)}, u32[]{:S(2)}, u32[]{:S(2)}) collective-permute-start(bf16[4,8,8,128]{3,2,1,0:T(8,128)(2,1)S(1)} %get-tuple-element.592), channel_id=1, source_target_pairs={{0,32},{32,64},{64,96},{96,128},{128,160},{160,192},{192,224},{1,3... | collective-permute-start | bytes 196616 | tf_op jit(solution)/shard_map/while/body/eval_jaxpr/ppermute | solution.py:15
  90.6 5.6 %collective-permute-start = (bf16[4,8,8,128]{3,2,1,0:T(8,128)(2,1)S(1)}, bf16[4,8,8,128]{3,2,1,0:T(8,128)(2,1)S(1)}, u32[]{:S(2)}, u32[]{:S(2)}) collective-permute-start(bf16[4,8,8,128]{3,2,1,0:T(8,128)(2,1)S(1)} %get-tuple-element.592), channel_id=1, source_target_pairs={{0,32},{32,64},{64,96},{96,128},{128,160},{160,192},{192,224},{1,3... | collective-permute-start | bytes 196616 | tf_op jit(solution)/shard_map/while/body/eval_jaxpr/ppermute | solution.py:15
  101.2 5.6 %collective-permute-start = (bf16[4,8,8,128]{3,2,1,0:T(8,128)(2,1)S(1)}, bf16[4,8,8,128]{3,2,1,0:T(8,128)(2,1)S(1)}, u32[]{:S(2)}, u32[]{:S(2)}) collective-permute-start(bf16[4,8,8,128]{3,2,1,0:T(8,128)(2,1)S(1)} %get-tuple-element.592), channel_id=1, source_target_pairs={{0,32},{32,64},{64,96},{96,128},{128,160},{160,192},{192,224},{1,3... | collective-permute-start | bytes 196616 | tf_op jit(solution)/shard_map/while/body/eval_jaxpr/ppermute | solution.py:15
  111.8 5.6 %collective-permute-start = (bf16[4,8,8,128]{3,2,1,0:T(8,128)(2,1)S(1)}, bf16[4,8,8,128]{3,2,1,0:T(8,128)(2,1)S(1)}, u32[]{:S(2)}, u32[]{:S(2)}) collective-permute-start(bf16[4,8,8,128]{3,2,1,0:T(8,128)(2,1)S(1)} %get-tuple-element.592), channel_id=1, source_target_pairs={{0,32},{32,64},{64,96},{96,128},{128,160},{160,192},{192,224},{1,3... | collective-permute-start | bytes 196616 | tf_op jit(solution)/shard_map/while/body/eval_jaxpr/ppermute | solution.py:15
  122.5 5.6 %collective-permute-start = (bf16[4,8,8,128]{3,2,1,0:T(8,128)(2,1)S(1)}, bf16[4,8,8,128]{3,2,1,0:T(8,128)(2,1)S(1)}, u32[]{:S(2)}, u32[]{:S(2)}) collective-permute-start(bf16[4,8,8,128]{3,2,1,0:T(8,128)(2,1)S(1)} %get-tuple-element.592), channel_id=1, source_target_pairs={{0,32},{32,64},{64,96},{96,128},{128,160},{160,192},{192,224},{1,3... | collective-permute-start | bytes 196616 | tf_op jit(solution)/shard_map/while/body/eval_jaxpr/ppermute | solution.py:15
  133.1 5.6 %collective-permute-start = (bf16[4,8,8,128]{3,2,1,0:T(8,128)(2,1)S(1)}, bf16[4,8,8,128]{3,2,1,0:T(8,128)(2,1)S(1)}, u32[]{:S(2)}, u32[]{:S(2)}) collective-permute-start(bf16[4,8,8,128]{3,2,1,0:T(8,128)(2,1)S(1)} %get-tuple-element.592), channel_id=1, source_target_pairs={{0,32},{32,64},{64,96},{96,128},{128,160},{160,192},{192,224},{1,3... | collective-permute-start | bytes 196616 | tf_op jit(solution)/shard_map/while/body/eval_jaxpr/ppermute | solution.py:15
  143.7 5.6 %collective-permute-start = (bf16[4,8,8,128]{3,2,1,0:T(8,128)(2,1)S(1)}, bf16[4,8,8,128]{3,2,1,0:T(8,128)(2,1)S(1)}, u32[]{:S(2)}, u32[]{:S(2)}) collective-permute-start(bf16[4,8,8,128]{3,2,1,0:T(8,128)(2,1)S(1)} %get-tuple-element.592), channel_id=1, source_target_pairs={{0,32},{32,64},{64,96},{96,128},{128,160},{160,192},{192,224},{1,3... | collective-permute-start | bytes 196616 | tf_op jit(solution)/shard_map/while/body/eval_jaxpr/ppermute | solution.py:15
  154.4 5.6 %collective-permute-start = (bf16[4,8,8,128]{3,2,1,0:T(8,128)(2,1)S(1)}, bf16[4,8,8,128]{3,2,1,0:T(8,128)(2,1)S(1)}, u32[]{:S(2)}, u32[]{:S(2)}) collective-permute-start(bf16[4,8,8,128]{3,2,1,0:T(8,128)(2,1)S(1)} %get-tuple-element.592), channel_id=1, source_target_pairs={{0,32},{32,64},{64,96},{96,128},{128,160},{160,192},{192,224},{1,3... | collective-permute-start | bytes 196616 | tf_op jit(solution)/shard_map/while/body/eval_jaxpr/ppermute | solution.py:15
  165.0 5.6 %collective-permute-start = (bf16[4,8,8,128]{3,2,1,0:T(8,128)(2,1)S(1)}, bf16[4,8,8,128]{3,2,1,0:T(8,128)(2,1)S(1)}, u32[]{:S(2)}, u32[]{:S(2)}) collective-permute-start(bf16[4,8,8,128]{3,2,1,0:T(8,128)(2,1)S(1)} %get-tuple-element.592), channel_id=1, source_target_pairs={{0,32},{32,64},{64,96},{96,128},{128,160},{160,192},{192,224},{1,3... | collective-permute-start | bytes 196616 | tf_op jit(solution)/shard_map/while/body/eval_jaxpr/ppermute | solution.py:15
  175.6 5.6 %collective-permute-start = (bf16[4,8,8,128]{3,2,1,0:T(8,128)(2,1)S(1)}, bf16[4,8,8,128]{3,2,1,0:T(8,128)(2,1)S(1)}, u32[]{:S(2)}, u32[]{:S(2)}) collective-permute-start(bf16[4,8,8,128]{3,2,1,0:T(8,128)(2,1)S(1)} %get-tuple-element.592), channel_id=1, source_target_pairs={{0,32},{32,64},{64,96},{96,128},{128,160},{160,192},{192,224},{1,3... | collective-permute-start | bytes 196616 | tf_op jit(solution)/shard_map/while/body/eval_jaxpr/ppermute | solution.py:15
  186.3 5.6 %collective-permute-start = (bf16[4,8,8,128]{3,2,1,0:T(8,128)(2,1)S(1)}, bf16[4,8,8,128]{3,2,1,0:T(8,128)(2,1)S(1)}, u32[]{:S(2)}, u32[]{:S(2)}) collective-permute-start(bf16[4,8,8,128]{3,2,1,0:T(8,128)(2,1)S(1)} %get-tuple-element.592), channel_id=1, source_target_pairs={{0,32},{32,64},{64,96},{96,128},{128,160},{160,192},{192,224},{1,3... | collective-permute-start | bytes 196616 | tf_op jit(solution)/shard_map/while/body/eval_jaxpr/ppermute | solution.py:15
  208.6 6.2 %collective-permute-start.1 = (bf16[4,8,8,128]{3,2,1,0:T(8,128)(2,1)}, bf16[4,8,8,128]{3,2,1,0:T(8,128)(2,1)}, u32[]{:S(2)}, u32[]{:S(2)}) collective-permute-start(bf16[4,8,8,128]{3,2,1,0:T(8,128)(2,1)} %get-tuple-element.630), channel_id=1, source_target_pairs={{32,0},{64,32},{96,64},{128,96},{160,128},{192,160},{224,192},{33,... | collective-permute-start | bytes 196616 | tf_op jit(solution)/shard_map/while/body/eval_jaxpr/ppermute | solution.py:15
  220.1 8.9 %collective-permute-start.1 = (bf16[4,8,8,128]{3,2,1,0:T(8,128)(2,1)}, bf16[4,8,8,128]{3,2,1,0:T(8,128)(2,1)}, u32[]{:S(2)}, u32[]{:S(2)}) collective-permute-start(bf16[4,8,8,128]{3,2,1,0:T(8,128)(2,1)} %get-tuple-element.630), channel_id=1, source_target_pairs={{32,0},{64,32},{96,64},{128,96},{160,128},{192,160},{224,192},{33,... | collective-permute-start | bytes 196616 | tf_op jit(solution)/shard_map/while/body/eval_jaxpr/ppermute | solution.py:15
  234.3 6.0 %collective-permute-start.1 = (bf16[4,8,8,128]{3,2,1,0:T(8,128)(2,1)}, bf16[4,8,8,128]{3,2,1,0:T(8,128)(2,1)}, u32[]{:S(2)}, u32[]{:S(2)}) collective-permute-start(bf16[4,8,8,128]{3,2,1,0:T(8,128)(2,1)} %get-tuple-element.630), channel_id=1, source_target_pairs={{32,0},{64,32},{96,64},{128,96},{160,128},{192,160},{224,192},{33,... | collective-permute-start | bytes 196616 | tf_op jit(solution)/shard_map/while/body/eval_jaxpr/ppermute | solution.py:15
  245.6 7.1 %collective-permute-start.1 = (bf16[4,8,8,128]{3,2,1,0:T(8,128)(2,1)}, bf16[4,8,8,128]{3,2,1,0:T(8,128)(2,1)}, u32[]{:S(2)}, u32[]{:S(2)}) collective-permute-start(bf16[4,8,8,128]{3,2,1,0:T(8,128)(2,1)} %get-tuple-element.630), channel_id=1, source_target_pairs={{32,0},{64,32},{96,64},{128,96},{160,128},{192,160},{224,192},{33,... | collective-permute-start | bytes 196616 | tf_op jit(solution)/shard_map/while/body/eval_jaxpr/ppermute | solution.py:15
  258.0 6.0 %collective-permute-start.1 = (bf16[4,8,8,128]{3,2,1,0:T(8,128)(2,1)}, bf16[4,8,8,128]{3,2,1,0:T(8,128)(2,1)}, u32[]{:S(2)}, u32[]{:S(2)}) collective-permute-start(bf16[4,8,8,128]{3,2,1,0:T(8,128)(2,1)} %get-tuple-element.630), channel_id=1, source_target_pairs={{32,0},{64,32},{96,64},{128,96},{160,128},{192,160},{224,192},{33,... | collective-permute-start | bytes 196616 | tf_op jit(solution)/shard_map/while/body/eval_jaxpr/ppermute | solution.py:15
  269.3 6.0 %collective-permute-start.1 = (bf16[4,8,8,128]{3,2,1,0:T(8,128)(2,1)}, bf16[4,8,8,128]{3,2,1,0:T(8,128)(2,1)}, u32[]{:S(2)}, u32[]{:S(2)}) collective-permute-start(bf16[4,8,8,128]{3,2,1,0:T(8,128)(2,1)} %get-tuple-element.630), channel_id=1, source_target_pairs={{32,0},{64,32},{96,64},{128,96},{160,128},{192,160},{224,192},{33,... | collective-permute-start | bytes 196616 | tf_op jit(solution)/shard_map/while/body/eval_jaxpr/ppermute | solution.py:15
  280.6 6.0 %collective-permute-start.1 = (bf16[4,8,8,128]{3,2,1,0:T(8,128)(2,1)}, bf16[4,8,8,128]{3,2,1,0:T(8,128)(2,1)}, u32[]{:S(2)}, u32[]{:S(2)}) collective-permute-start(bf16[4,8,8,128]{3,2,1,0:T(8,128)(2,1)} %get-tuple-element.630), channel_id=1, source_target_pairs={{32,0},{64,32},{96,64},{128,96},{160,128},{192,160},{224,192},{33,... | collective-permute-start | bytes 196616 | tf_op jit(solution)/shard_map/while/body/eval_jaxpr/ppermute | solution.py:15
  291.9 6.0 %collective-permute-start.1 = (bf16[4,8,8,128]{3,2,1,0:T(8,128)(2,1)}, bf16[4,8,8,128]{3,2,1,0:T(8,128)(2,1)}, u32[]{:S(2)}, u32[]{:S(2)}) collective-permute-start(bf16[4,8,8,128]{3,2,1,0:T(8,128)(2,1)} %get-tuple-element.630), channel_id=1, source_target_pairs={{32,0},{64,32},{96,64},{128,96},{160,128},{192,160},{224,192},{33,... | collective-permute-start | bytes 196616 | tf_op jit(solution)/shard_map/while/body/eval_jaxpr/ppermute | solution.py:15
  303.2 6.0 %collective-permute-start.1 = (bf16[4,8,8,128]{3,2,1,0:T(8,128)(2,1)}, bf16[4,8,8,128]{3,2,1,0:T(8,128)(2,1)}, u32[]{:S(2)}, u32[]{:S(2)}) collective-permute-start(bf16[4,8,8,128]{3,2,1,0:T(8,128)(2,1)} %get-tuple-element.630), channel_id=1, source_target_pairs={{32,0},{64,32},{96,64},{128,96},{160,128},{192,160},{224,192},{33,... | collective-permute-start | bytes 196616 | tf_op jit(solution)/shard_map/while/body/eval_jaxpr/ppermute | solution.py:15
  314.5 6.0 %collective-permute-start.1 = (bf16[4,8,8,128]{3,2,1,0:T(8,128)(2,1)}, bf16[4,8,8,128]{3,2,1,0:T(8,128)(2,1)}, u32[]{:S(2)}, u32[]{:S(2)}) collective-permute-start(bf16[4,8,8,128]{3,2,1,0:T(8,128)(2,1)} %get-tuple-element.630), channel_id=1, source_target_pairs={{32,0},{64,32},{96,64},{128,96},{160,128},{192,160},{224,192},{33,... | collective-permute-start | bytes 196616 | tf_op jit(solution)/shard_map/while/body/eval_jaxpr/ppermute | solution.py:15
  325.8 6.0 %collective-permute-start.1 = (bf16[4,8,8,128]{3,2,1,0:T(8,128)(2,1)}, bf16[4,8,8,128]{3,2,1,0:T(8,128)(2,1)}, u32[]{:S(2)}, u32[]{:S(2)}) collective-permute-start(bf16[4,8,8,128]{3,2,1,0:T(8,128)(2,1)} %get-tuple-element.630), channel_id=1, source_target_pairs={{32,0},{64,32},{96,64},{128,96},{160,128},{192,160},{224,192},{33,... | collective-permute-start | bytes 196616 | tf_op jit(solution)/shard_map/while/body/eval_jaxpr/ppermute | solution.py:15
  337.1 6.0 %collective-permute-start.1 = (bf16[4,8,8,128]{3,2,1,0:T(8,128)(2,1)}, bf16[4,8,8,128]{3,2,1,0:T(8,128)(2,1)}, u32[]{:S(2)}, u32[]{:S(2)}) collective-permute-start(bf16[4,8,8,128]{3,2,1,0:T(8,128)(2,1)} %get-tuple-element.630), channel_id=1, source_target_pairs={{32,0},{64,32},{96,64},{128,96},{160,128},{192,160},{224,192},{33,... | collective-permute-start | bytes 196616 | tf_op jit(solution)/shard_map/while/body/eval_jaxpr/ppermute | solution.py:15
  348.4 6.0 %collective-permute-start.1 = (bf16[4,8,8,128]{3,2,1,0:T(8,128)(2,1)}, bf16[4,8,8,128]{3,2,1,0:T(8,128)(2,1)}, u32[]{:S(2)}, u32[]{:S(2)}) collective-permute-start(bf16[4,8,8,128]{3,2,1,0:T(8,128)(2,1)} %get-tuple-element.630), channel_id=1, source_target_pairs={{32,0},{64,32},{96,64},{128,96},{160,128},{192,160},{224,192},{33,... | collective-permute-start | bytes 196616 | tf_op jit(solution)/shard_map/while/body/eval_jaxpr/ppermute | solution.py:15
  359.7 6.0 %collective-permute-start.1 = (bf16[4,8,8,128]{3,2,1,0:T(8,128)(2,1)}, bf16[4,8,8,128]{3,2,1,0:T(8,128)(2,1)}, u32[]{:S(2)}, u32[]{:S(2)}) collective-permute-start(bf16[4,8,8,128]{3,2,1,0:T(8,128)(2,1)} %get-tuple-element.630), channel_id=1, source_target_pairs={{32,0},{64,32},{96,64},{128,96},{160,128},{192,160},{224,192},{33,... | collective-permute-start | bytes 196616 | tf_op jit(solution)/shard_map/while/body/eval_jaxpr/ppermute | solution.py:15
  371.0 6.0 %collective-permute-start.1 = (bf16[4,8,8,128]{3,2,1,0:T(8,128)(2,1)}, bf16[4,8,8,128]{3,2,1,0:T(8,128)(2,1)}, u32[]{:S(2)}, u32[]{:S(2)}) collective-permute-start(bf16[4,8,8,128]{3,2,1,0:T(8,128)(2,1)} %get-tuple-element.630), channel_id=1, source_target_pairs={{32,0},{64,32},{96,64},{128,96},{160,128},{192,160},{224,192},{33,... | collective-permute-start | bytes 196616 | tf_op jit(solution)/shard_map/while/body/eval_jaxpr/ppermute | solution.py:15
  498.3 10.7 %collective-permute-start.2 = (bf16[112,128]{1,0:T(8,128)(2,1)S(1)}, bf16[112,128]{1,0:T(8,128)(2,1)S(1)}, u32[]{:S(2)}, u32[]{:S(2)}) collective-permute-start(bf16[112,128]{1,0:T(8,128)(2,1)S(1)} %fusion), channel_id=1, source_target_pairs={{0,1},{1,2},{2,3},{3,4},{4,5},{5,6},{6,7},{7,8},{8,9},{9,10},{10,1... | collective-permute-start | bytes 86024
  500.3 7.6 %collective-permute-start.3 = (bf16[12,128]{1,0:T(8,128)(2,1)S(1)}, bf16[12,128]{1,0:T(8,128)(2,1)S(1)}, u32[]{:S(2)}, u32[]{:S(2)}) collective-permute-start(bf16[12,128]{1,0:T(8,128)(2,1)S(1)} %slice.589), channel_id=1, source_target_pairs={{0,2},{1,3},{2,4},{3,5},{4,6},{5,7},{6,8},{7,9},{8,10},{9,11},{10,... | collective-permute-start | bytes 9224
  (18 other events, 174.3 us)
